TPU v7x, 32 devices: a whole 2x2x4 slice. The times are simulated.
32 devices in a mesh: dp: 8 (over z, y), tensor: 4 (over x, core).
Axes of the slice: x: 2, y: 2, z: 4, core: 2. Of those that a mesh axis runs over, the one named last changes fastest.
Arguments:
- tokens: bfloat16 [8192, 1024], P(('dp', 'tensor')), may hold values from -6 to 6
- cotangent: float32 [8192, 1024], P(('dp', 'tensor')), may hold values from -6 to 6
- lengths: int32 [8, 2], P('dp'), may hold values from 64 to 512, as said below
- order: int32 [8, 1024], P('dp'), may hold values from 0 to 1023, each once within a row
- adapter_ids: int32 [8, 2], P('dp'), may hold values from 0 to 7
- norm1_gain: float32 [1024], replicated, may hold values from 0.25 to 1.75
- norm1_shift: float32 [1024], replicated, may hold values from -1.5 to 1.5
- qkv_weight: bfloat16 [1024, 3, 1024], P(None, None, 'tensor'), may hold values from -0.1875 to 0.1875
- qv_bias: float32 [2, 1024], P(None, 'tensor'), may hold values from -1.5 to 1.5
- proj_weight: bfloat16 [1024, 1024], P('tensor'), may hold values from -1.5 to 1.5
- proj_bias: float32 [1024], replicated, may hold values from -1.5 to 1.5
- norm2_gain: float32 [1024], replicated, may hold values from 0.25 to 1.75
- norm2_shift: float32 [1024], replicated, may hold values from -1.5 to 1.5
- up_weight: bfloat16 [1024, 4096], P(None, 'tensor'), may hold values from -0.1875 to 0.1875
- up_bias: float32 [4096], P('tensor'), may hold values from -1.5 to 1.5
- down_weight: bfloat16 [4096, 1024], P('tensor'), may hold values from -0.09375 to 0.09375
- down_bias: float32 [1024], replicated, may hold values from -1.5 to 1.5
- adapt_qkv_in: bfloat16 [1024, 128], replicated, may hold values from -0.1875 to 0.1875
- adapt_qkv_out: bfloat16 [128, 3, 1024], P(None, None, 'tensor'), may hold values from -0.75 to 0.75
- adapt_proj_in: bfloat16 [1024, 128], P('tensor'), may hold values from -0.75 to 0.75
- adapt_proj_out: bfloat16 [128, 1024], replicated, may hold values from -0.75 to 0.75
- adapt_up_in: bfloat16 [1024, 128], replicated, may hold values from -0.1875 to 0.1875
- adapt_up_out: bfloat16 [128, 4096], P(None, 'tensor'), may hold values from -0.75 to 0.75
- adapt_down_in: bfloat16 [4096, 128], P('tensor'), may hold values from -0.09375 to 0.09375
- adapt_down_out: bfloat16 [128, 1024], replicated, may hold values from -0.75 to 0.75
Outputs:
- result: float32 [8192, 1024], P(('dp', 'tensor'))
- grad_input: float32 [8192, 1024], P(('dp', 'tensor'))
- grad_qkv_in: float32 [1024, 128], replicated
- grad_qkv_out: float32 [128, 3, 1024], P(None, None, 'tensor')
- grad_proj_in: float32 [1024, 128], P('tensor')
- grad_proj_out: float32 [128, 1024], replicated
- grad_up_in: float32 [1024, 128], replicated
- grad_up_out: float32 [128, 4096], P(None, 'tensor')
- grad_down_in: float32 [4096, 128], P('tensor')
- grad_down_out: float32 [128, 1024], replicated
Inputs may be any that keep to these rules, and one draw needn't show every extreme that they name: `lengths`: in every group one sequence has exactly 512 valid tokens; the others have at least 512 // 8 (and at least one). `order`: each row is a permutation of the group's 1024 stored rows.
All inputs are finite; a program needn't handle non-finite values.
Results may differ from a plain program's by a relative error of at most 0.023.
Values may be sent and summed in bfloat16 or wider, within the bound.
No kernel may reach another device: no remote copies, remote signals or barrier semaphores. Data moves between devices by JAX's collectives and lax.ppermute only.
A program may use at most 128 MiB of HBM per device.

v0:
```python
import math
import jax
import jax.numpy as jnp
from jax import lax
from jax.sharding import PartitionSpec as P

D = 1024
HD = 64
RANK = 16
EPSILON = 1e-05
NEGATIVE = -1000000000.0


def layer_norm(values, gain, shift):
    centre = values - jnp.mean(values, -1, keepdims=True)
    spread = jnp.mean(centre * centre, -1, keepdims=True)
    return centre * lax.rsqrt(spread + EPSILON) * gain + shift


def matmul(left, right):
    return jnp.dot(left, right, preferred_element_type=jnp.float32)


def matmul_back(left, right):
    return lax.dot_general(
        left, right, (((1,), (1,)), ((), ())), preferred_element_type=jnp.float32
    )


def matmul_over(left, right):
    return lax.dot_general(
        left, right, (((0,), (0,)), ((), ())), preferred_element_type=jnp.float32
    )


def gelu_tanh(values):
    return jax.nn.gelu(values, approximate=True)


def block_scores(queries, keys, query_start, length):
    scale = 1.0 / math.sqrt(HD)
    scores = jnp.einsum("qhc,khc->hqk", queries, keys, preferred_element_type=jnp.float32) * scale
    query_pos = query_start + jnp.arange(queries.shape[0], dtype=jnp.int32)
    key_pos = jnp.arange(keys.shape[0], dtype=jnp.int32)
    allowed = (key_pos[None, :] <= query_pos[:, None]) & (key_pos[None, :] < length)
    return jnp.where(allowed[None], scores, NEGATIVE)


def attention_forward(qkv_seq, lengths_row, seq_len):
    group_rows = qkv_seq.shape[0]
    heads_here = qkv_seq.shape[2] // HD
    block_rows = min(512, seq_len)
    per_seq = seq_len // block_rows
    split = qkv_seq.reshape(group_rows, 3, heads_here, HD)

    def one_block(block_id):
        seq_id = block_id // per_seq
        query_start = block_id % per_seq * block_rows
        base = seq_id * seq_len
        queries = lax.dynamic_slice_in_dim(split[:, 0], base + query_start, block_rows, 0)
        keys = lax.dynamic_slice_in_dim(split[:, 1], base, seq_len, 0)
        values = lax.dynamic_slice_in_dim(split[:, 2], base, seq_len, 0)
        scores = block_scores(queries, keys, query_start, lengths_row[seq_id])
        top = jnp.max(scores, -1, keepdims=True)
        weights = jnp.exp(scores - top)
        total = jnp.sum(weights, -1, keepdims=True)
        probs = (weights / total).astype(jnp.bfloat16)
        attended = jnp.einsum("hqk,khc->qhc", probs, values, preferred_element_type=jnp.float32)
        return (attended.reshape(block_rows, heads_here * HD), (top + jnp.log(total))[..., 0])

    blocks = group_rows // block_rows
    outputs, log_totals = lax.map(one_block, jnp.arange(blocks, dtype=jnp.int32))
    return (outputs.reshape(group_rows, heads_here * HD), log_totals)


def attention_backward(qkv_seq, grad_seq, log_totals, lengths_row, seq_len):
    group_rows = qkv_seq.shape[0]
    heads_here = qkv_seq.shape[2] // HD
    block_rows = min(512, seq_len)
    per_seq = seq_len // block_rows
    seqs = group_rows // seq_len
    scale = 1.0 / math.sqrt(HD)
    split = qkv_seq.reshape(group_rows, 3, heads_here, HD)
    grad_split = grad_seq.reshape(group_rows, heads_here, HD)

    def one_block(block_id):
        seq_id = block_id // per_seq
        query_start = block_id % per_seq * block_rows
        base = seq_id * seq_len
        queries = lax.dynamic_slice_in_dim(split[:, 0], base + query_start, block_rows, 0)
        keys = lax.dynamic_slice_in_dim(split[:, 1], base, seq_len, 0)
        values = lax.dynamic_slice_in_dim(split[:, 2], base, seq_len, 0)
        grad_block = lax.dynamic_slice_in_dim(grad_split, base + query_start, block_rows, 0)
        scores = block_scores(queries, keys, query_start, lengths_row[seq_id])
        probs = jnp.exp(scores - log_totals[block_id][..., None])
        grad_probs = jnp.einsum(
            "qhc,khc->hqk", grad_block, values, preferred_element_type=jnp.float32
        )
        centre = jnp.sum(probs * grad_probs, -1, keepdims=True)
        grad_raw = (probs * (grad_probs - centre) * scale).astype(jnp.bfloat16)
        grad_query = jnp.einsum("hqk,khc->qhc", grad_raw, keys, preferred_element_type=jnp.float32)
        grad_key = jnp.einsum("hqk,qhc->khc", grad_raw, queries, preferred_element_type=jnp.float32)
        grad_value = jnp.einsum(
            "hqk,qhc->khc",
            probs.astype(jnp.bfloat16),
            grad_block,
            preferred_element_type=jnp.float32,
        )
        return (grad_query, grad_key, grad_value)

    blocks = group_rows // block_rows
    grad_query, grad_key, grad_value = lax.map(one_block, jnp.arange(blocks, dtype=jnp.int32))
    width_here = heads_here * HD
    grad_query = grad_query.reshape(group_rows, width_here)
    grad_key = jnp.sum(grad_key.reshape(seqs, per_seq, seq_len, width_here), axis=1).reshape(
        group_rows, width_here
    )
    grad_value = jnp.sum(grad_value.reshape(seqs, per_seq, seq_len, width_here), axis=1).reshape(
        group_rows, width_here
    )
    return jnp.stack([grad_query, grad_key, grad_value], 1)


def body(
    tokens,
    cotangent,
    lengths,
    order,
    adapter_ids,
    norm1_gain,
    norm1_shift,
    qkv_weight,
    qv_bias,
    proj_weight,
    proj_bias,
    norm2_gain,
    norm2_shift,
    up_weight,
    up_bias,
    down_weight,
    down_bias,
    adapt_qkv_in,
    adapt_qkv_out,
    adapt_proj_in,
    adapt_proj_out,
    adapt_up_in,
    adapt_up_out,
    adapt_down_in,
    adapt_down_out,
):
    own_rows = tokens.shape[0]
    order_row = order[0]
    lengths_row = lengths[0]
    ids_row = adapter_ids[0]
    group_rows = order_row.shape[0]
    seqs = lengths_row.shape[0]
    seq_len = group_rows // seqs
    adapt_cols = adapt_qkv_in.shape[1]
    rank_index = lax.axis_index("tensor")
    inverse = (
        jnp.zeros((group_rows,), jnp.int32)
        .at[order_row]
        .set(jnp.arange(group_rows, dtype=jnp.int32))
    )
    seq_of = inverse // seq_len
    adapter_of = jnp.sum(
        jnp.where(
            seq_of[:, None] == jnp.arange(seqs, dtype=jnp.int32)[None, :], ids_row[None, :], 0
        ),
        axis=1,
    )
    group_mask = (
        jnp.arange(adapt_cols, dtype=jnp.int32)[None, :] // RANK == adapter_of[:, None]
    ).astype(jnp.float32)
    own_mask = lax.dynamic_slice_in_dim(group_mask, rank_index * own_rows, own_rows, 0)
    bias_three = jnp.stack([qv_bias[0], jnp.zeros_like(qv_bias[0]), qv_bias[1]])
    proj_joined = jnp.concatenate([proj_weight, adapt_proj_in], 1)
    down_joined = jnp.concatenate([down_weight, adapt_down_in], 1)
    up_joined = jnp.concatenate([up_weight, adapt_up_out], 0)
    qkv_joined = jnp.concatenate([qkv_weight, adapt_qkv_out], 0)

    def project_qkv(rows_all, lowrank_all):
        value = jnp.einsum("rd,dkc->rkc", rows_all, qkv_weight, preferred_element_type=jnp.float32)
        value = value + jnp.einsum(
            "ra,akc->rkc", lowrank_all, adapt_qkv_out, preferred_element_type=jnp.float32
        )
        return (value + bias_three[None]).astype(jnp.bfloat16)

    def project_up(rows_all, lowrank_all):
        return matmul(rows_all, up_weight) + matmul(lowrank_all, adapt_up_out) + up_bias

    inputs = tokens.astype(jnp.float32)
    normed1 = layer_norm(inputs, norm1_gain, norm1_shift).astype(jnp.bfloat16)
    low1 = (matmul(normed1, adapt_qkv_in) * own_mask).astype(jnp.bfloat16)
    normed1_all, low1_small = (
        lax.all_gather(normed1, "tensor", axis=0, tiled=True),
        lax.all_gather(low1, "tensor", axis=0, tiled=True),
    )
    low1_all = low1_small
    qkv_arr = project_qkv(normed1_all, low1_all)
    qkv_seq = jnp.take(qkv_arr, order_row, axis=0)
    attended_seq, log_totals = attention_forward(qkv_seq, lengths_row, seq_len)
    attended = jnp.take(attended_seq.astype(jnp.bfloat16), inverse, axis=0)
    rows = attended
    mask_rows = group_mask
    part = matmul(rows, proj_joined)
    summed_attn = lax.psum_scatter(
        jnp.concatenate([part[:, :D], part[:, D:] * mask_rows], 1).astype(jnp.bfloat16),
        "tensor",
        scatter_dimension=0,
        tiled=True,
    ).astype(jnp.float32)
    proj_low = summed_attn[:, D:].astype(jnp.bfloat16)
    mid = inputs + summed_attn[:, :D] + matmul(proj_low, adapt_proj_out) + proj_bias
    normed2 = layer_norm(mid, norm2_gain, norm2_shift).astype(jnp.bfloat16)
    low2 = (matmul(normed2, adapt_up_in) * own_mask).astype(jnp.bfloat16)
    normed2_all, low2_small = (
        lax.all_gather(normed2, "tensor", axis=0, tiled=True),
        lax.all_gather(low2, "tensor", axis=0, tiled=True),
    )
    low2_all = low2_small
    upper = project_up(normed2_all, low2_all)
    active = gelu_tanh(upper).astype(jnp.bfloat16)
    rows = active
    mask_rows = group_mask
    part = matmul(rows, down_joined)
    summed_mlp = lax.psum_scatter(
        jnp.concatenate([part[:, :D], part[:, D:] * mask_rows], 1).astype(jnp.bfloat16),
        "tensor",
        scatter_dimension=0,
        tiled=True,
    ).astype(jnp.float32)
    down_low = summed_mlp[:, D:].astype(jnp.bfloat16)
    result = mid + summed_mlp[:, :D] + matmul(down_low, adapt_down_out) + down_bias
    grad_mlp = cotangent.astype(jnp.bfloat16)
    grad_down_low = (matmul_back(grad_mlp, adapt_down_out) * own_mask).astype(jnp.bfloat16)
    grad_down_out_part = matmul_over(down_low, grad_mlp)
    grad_mlp_all, grad_down_small = (
        lax.all_gather(grad_mlp, "tensor", axis=0, tiled=True),
        lax.all_gather(grad_down_low, "tensor", axis=0, tiled=True),
    )
    normed2_again, low2_again_small = (
        lax.all_gather(normed2, "tensor", axis=0, tiled=True),
        lax.all_gather(low2, "tensor", axis=0, tiled=True),
    )
    upper = project_up(normed2_again, low2_again_small)
    active = gelu_tanh(upper).astype(jnp.bfloat16)
    low2_all = low2_again_small
    grad_active = matmul_back(grad_mlp_all, down_weight) + matmul_back(
        grad_down_small, adapt_down_in
    )
    grad_down_in_part = matmul_over(active, grad_down_small)
    gelu_value, gelu_pull = jax.vjp(gelu_tanh, upper)
    grad_upper = gelu_pull(grad_active)[0].astype(jnp.bfloat16)
    grad_up_out_part = matmul_over(low2_all, grad_upper)
    rows = grad_upper
    part = matmul_back(rows, up_joined)
    summed_up = lax.psum_scatter(
        jnp.concatenate([part[:, :D], part[:, D:]], 1).astype(jnp.bfloat16),
        "tensor",
        scatter_dimension=0,
        tiled=True,
    ).astype(jnp.float32)
    grad_low2 = (summed_up[:, D:] * own_mask).astype(jnp.bfloat16)
    grad_up_in_part = matmul_over(normed2, grad_low2)
    grad_normed2 = summed_up[:, :D] + matmul_back(grad_low2, adapt_up_in)
    norm2_value, norm2_pull = jax.vjp(
        lambda values: layer_norm(values, norm2_gain, norm2_shift), mid
    )
    grad_mid = cotangent + norm2_pull(grad_normed2)[0]
    grad_attn = grad_mid.astype(jnp.bfloat16)
    grad_proj_low = (matmul_back(grad_attn, adapt_proj_out) * own_mask).astype(jnp.bfloat16)
    grad_proj_out_part = matmul_over(proj_low, grad_attn)
    grad_attn_all, grad_proj_small = (
        lax.all_gather(grad_attn, "tensor", axis=0, tiled=True),
        lax.all_gather(grad_proj_low, "tensor", axis=0, tiled=True),
    )
    grad_attended = matmul_back(grad_attn_all, proj_weight) + matmul_back(
        grad_proj_small, adapt_proj_in
    )
    grad_proj_in_part = matmul_over(attended, grad_proj_small)
    grad_attended_seq = jnp.take(grad_attended, order_row, axis=0).astype(jnp.bfloat16)
    normed1_again, low1_again_small = (
        lax.all_gather(normed1, "tensor", axis=0, tiled=True),
        lax.all_gather(low1, "tensor", axis=0, tiled=True),
    )
    qkv_seq = jnp.take(project_qkv(normed1_again, low1_again_small), order_row, axis=0)
    low1_all = low1_again_small
    grad_qkv_seq = attention_backward(qkv_seq, grad_attended_seq, log_totals, lengths_row, seq_len)
    grad_qkv = jnp.take(grad_qkv_seq.astype(jnp.bfloat16), inverse, axis=0)
    grad_qkv_out_part = jnp.einsum(
        "ra,rkc->akc", low1_all, grad_qkv, preferred_element_type=jnp.float32
    )
    rows = grad_qkv
    part = jnp.einsum("rkc,dkc->rd", rows, qkv_joined, preferred_element_type=jnp.float32)
    summed_qkv = lax.psum_scatter(
        jnp.concatenate([part[:, :D], part[:, D:]], 1).astype(jnp.bfloat16),
        "tensor",
        scatter_dimension=0,
        tiled=True,
    ).astype(jnp.float32)
    grad_low1 = (summed_qkv[:, D:] * own_mask).astype(jnp.bfloat16)
    grad_qkv_in_part = matmul_over(normed1, grad_low1)
    grad_normed1 = summed_qkv[:, :D] + matmul_back(grad_low1, adapt_qkv_in)
    norm1_value, norm1_pull = jax.vjp(
        lambda values: layer_norm(values, norm1_gain, norm1_shift), inputs
    )
    grad_input = grad_mid + norm1_pull(grad_normed1)[0]
    wide = lax.psum(
        (grad_qkv_in_part, grad_proj_out_part, grad_up_in_part, grad_down_out_part),
        ("dp", "tensor"),
    )
    narrow = (
        lax.psum(grad_qkv_out_part.astype(jnp.bfloat16), "dp").astype(jnp.float32),
        lax.psum(grad_proj_in_part.astype(jnp.bfloat16), "dp").astype(jnp.float32),
        lax.psum(grad_up_out_part.astype(jnp.bfloat16), "dp").astype(jnp.float32),
        lax.psum(grad_down_in_part.astype(jnp.bfloat16), "dp").astype(jnp.float32),
    )
    return (
        result,
        grad_input,
        wide[0],
        narrow[0],
        narrow[1],
        wide[1],
        wide[2],
        narrow[2],
        narrow[3],
        wide[3],
    )


def solution(mesh):
    in_specs = (
        P(("dp", "tensor"), None),
        P(("dp", "tensor"), None),
        P("dp", None),
        P("dp", None),
        P("dp", None),
        P(),
        P(),
        P(None, None, "tensor"),
        P(None, "tensor"),
        P("tensor", None),
        P(),
        P(),
        P(),
        P(None, "tensor"),
        P("tensor"),
        P("tensor", None),
        P(),
        P(),
        P(None, None, "tensor"),
        P("tensor", None),
        P(),
        P(),
        P(None, "tensor"),
        P("tensor", None),
        P(),
    )
    out_specs = (
        P(("dp", "tensor"), None),
        P(("dp", "tensor"), None),
        P(),
        P(None, None, "tensor"),
        P("tensor", None),
        P(),
        P(),
        P(None, "tensor"),
        P("tensor", None),
        P(),
    )
    return jax.shard_map(body, mesh=mesh, in_specs=in_specs, out_specs=out_specs, check_vma=False)
```

profile of v0, /device:TPU:0, one launch (start us, length us, event | category | flops | bytes accessed | tf_op | source)
XLA Modules:
  0.0 638.7 jit_solution(10005724395536461428)
XLA Ops:
  20.2 8.9 %all_gather.29 = bf16[1024,128]{1,0:T(8,128)(2,1)S(1)} all-gather(bf16[256,128]{1,0:T(8,128)(2,1)S(1)} %fusion.97), channel_id=1, replica_groups=mesh['dp'=8,'tensor'=4] {'tensor'}, dimensions={0}, use_global_device_ids=true | all-gather | bytes 327680 | tf_op jit(solution)/shard_map/all_gather | solution.py:197
  31.9 6.9 %all-gather.5.cloned.1.call-done = bf16[1024,1024]{1,0:T(8,128)(2,1)} async-done(((bf16[256,1024]{1,0:T(8,128)(2,1)}), bf16[1024,1024]{1,0:T(8,128)(2,1)}) %all-gather.5.cloned.1.call-update) | async-done | bytes 2097168 | tf_op jit(solution)/shard_map/all_gather | solution.py:196
  46.0 10.1 %gather_fusion.2 = bf16[1024,3,256]{2,1,0:T(4,128)(2,1)} fusion(bf16[1024,3,256]{2,1,0:T(4,128)(2,1)} %copy.65, s32[1024]{0:T(1024)S(1)} %fusion.129), kind=kCustom, calls=%fused_computation.clone | custom fusion | bytes 3149824 | tf_op jit(solution)/shard_map/jit(_take)/gather | solution.py:201
  56.1 6.3 broadcast_select_fusion.1
  65.3 15.9 %while.32 = (s32[]{:T(128)}, bf16[2,512,256]{1,2,0:T(8,128)(2,1)S(1)}, f32[2,4,512]{2,1,0:T(4,128)S(1)}, bf16[1024,3,4,64]{0,3,2,1:T(8,128)(2,1)S(1)}, s32[2]{0:...) while((s32[]{:T(128)}, ...), condition=%wide.region_7.9_spmd, body=%wide.region_4.8_spmd.sunk | while | flops 281541120 | bytes 18417900 | solution.py:72
  91.6 32.2 %reduce-scatter.5.cloned.1.call-done = bf16[256,1152]{1,0:T(8,128)(2,1)} async-done(((bf16[1024,1152]{1,0:T(8,128)(2,1)}), bf16[256,1152]{1,0:T(8,128)(2,1)}) %reduce-scatter.5.cloned.1.call-update) | async-done | bytes 589840 | tf_op jit(solution)/shard_map/reduce_scatter | solution.py:207
  129.0 6.4 %all_gather.33 = bf16[1024,128]{1,0:T(8,128)(2,1)} all-gather(bf16[256,128]{1,0:T(8,128)(2,1)S(1)} %fusion.99), channel_id=1, replica_groups=mesh['dp'=8,'tensor'=4] {'tensor'}, dimensions={0}, use_global_device_ids=true | all-gather | bytes 327680 | tf_op jit(solution)/shard_map/all_gather | solution.py:240
  135.4 13.3 %all-gather.9.cloned.1.call-done = bf16[1024,1024]{1,0:T(8,128)(2,1)} async-done(((bf16[256,1024]{1,0:T(8,128)(2,1)}), bf16[1024,1024]{1,0:T(8,128)(2,1)}) %all-gather.9.cloned.1.call-update) | async-done | bytes 2097168 | tf_op jit(solution)/shard_map/all_gather | solution.py:239
  148.7 6.6 %fusion.153 = f32[1024,1024]{1,0:T(8,128)} fusion(bf16[1024,1024]{1,0:T(8,128)(2,1)} %all-gather.9.cloned.1.call-done, bf16[1024,1024]{1,0:T(8,128)(2,1)} %param.46), kind=kOutput, calls=%fused_computation.219 | convolution fusion | flops 2147483648 | bytes 8388608 | tf_op jit(solution)/shard_map/dot_general | solution.py:25
  155.6 5.8 all_gather.31
  161.4 12.0 %all-gather.7.cloned.1.call-done = bf16[1024,1024]{1,0:T(8,128)(2,1)} async-done(((bf16[256,1024]{1,0:T(8,128)(2,1)}), bf16[1024,1024]{1,0:T(8,128)(2,1)}) %all-gather.7.cloned.1.call-update) | async-done | bytes 2097168 | tf_op jit(solution)/shard_map/all_gather | solution.py:218
  190.7 33.2 %reduce-scatter.9.cloned.1.call-done = bf16[256,1152]{1,0:T(8,128)(2,1)} async-done(((bf16[1024,1152]{1,0:T(8,128)(2,1)}), bf16[256,1152]{1,0:T(8,128)(2,1)}) %reduce-scatter.9.cloned.1.call-update) | async-done | bytes 589840 | tf_op jit(solution)/shard_map/reduce_scatter | solution.py:258
  229.6 6.5 %fusion.77 = bf16[1024,1152]{1,0:T(8,128)(2,1)S(1)} fusion(bf16[1024,128]{1,0:T(8,128)(2,1)S(1)} %copy-done.64, bf16[1024,1024]{1,0:T(8,128)(2,1)} %param.46, f32[1024,1024]{1,0:T(8,128)} %copy-done.18), kind=kOutput, calls=%fused_computation.87 | convolution fusion | flops 2430074880 | bytes 8912896 | tf_op jit(solution)/shard_map/dot_general | solution.py:21
  246.1 6.3 all_gather.35
  266.1 62.1 %while.33 = (s32[]{:T(128)}, bf16[2,512,4,64]{1,3,2,0:T(8,128)(2,1)}, bf16[2,512,4,64]{1,3,2,0:T(8,128)(2,1)}, bf16[2,512,4,64]{1,3,2,0:T(8,128)(2,1)}, bf16[102...) while((s32[]{:T(128)}, ...), condition=%wide.region_17.19_spmd, body=%wide.region_15.18_spmd.sunk | while | flops 686298624 | bytes 57437636 | solution.py:112
  277.6 7.9 %fusion.232 = bf16[2,512,4,64]{1,3,2,0:T(8,128)(2,1)} fusion(bf16[2,512,4,64]{1,3,2,0:T(8,128)(2,1)} %get-tuple-element.493, s32[]{:T(128)S(6)} %copy.112, f32[4,512,512]{1,2,0:T(8,128)} %subtract_exponential_fusion.3, f32[4,512,512]{1,2,0:T(8,128)} %fusion.230, bf16[1024,1,4,64]{0,3,2,1:T(8,128)(2,1)} %copy-done.5, s32[]{:T(128)S(6)} %select_n.203), kind=kOutput, calls=%fused_computation.43.clone.1 | convolution fusion | flops 139463168 | bytes 17563656 | tf_op jit(solution)/shard_map/while/body/eval_jaxpr/hqk,qhc->khc/dot_general | solution.py:102
  285.6 8.0 %fusion.231 = bf16[2,512,4,64]{1,3,2,0:T(8,128)(2,1)} fusion(bf16[2,512,4,64]{1,3,2,0:T(8,128)(2,1)} %get-tuple-element.492, s32[]{:T(128)S(6)} %copy.112, f32[4,512,512]{1,2,0:T(8,128)} %subtract_exponential_fusion.3, f32[4,512,512]{1,2,0:T(8,128)} %fusion.230, bf16[1024,1,4,64]{0,3,2,1:T(8,128)(2,1)} %copy-done.4, s32[]{:T(128)S(6)} %select_n.203), kind=kOutput, calls=%fused_computation.41.clone.1 | convolution fusion | flops 139463168 | bytes 17563656 | tf_op jit(solution)/shard_map/while/body/eval_jaxpr/hqk,khc->qhc/dot_general | solution.py:101
  308.7 7.9 %fusion.232 = bf16[2,512,4,64]{1,3,2,0:T(8,128)(2,1)} fusion(bf16[2,512,4,64]{1,3,2,0:T(8,128)(2,1)} %get-tuple-element.493, s32[]{:T(128)S(6)} %copy.112, f32[4,512,512]{1,2,0:T(8,128)} %subtract_exponential_fusion.3, f32[4,512,512]{1,2,0:T(8,128)} %fusion.230, bf16[1024,1,4,64]{0,3,2,1:T(8,128)(2,1)} %copy-done.5, s32[]{:T(128)S(6)} %select_n.203), kind=kOutput, calls=%fused_computation.43.clone.1 | convolution fusion | flops 139463168 | bytes 17563656 | tf_op jit(solution)/shard_map/while/body/eval_jaxpr/hqk,qhc->khc/dot_general | solution.py:102
  316.6 8.0 %fusion.231 = bf16[2,512,4,64]{1,3,2,0:T(8,128)(2,1)} fusion(bf16[2,512,4,64]{1,3,2,0:T(8,128)(2,1)} %get-tuple-element.492, s32[]{:T(128)S(6)} %copy.112, f32[4,512,512]{1,2,0:T(8,128)} %subtract_exponential_fusion.3, f32[4,512,512]{1,2,0:T(8,128)} %fusion.230, bf16[1024,1,4,64]{0,3,2,1:T(8,128)(2,1)} %copy-done.4, s32[]{:T(128)S(6)} %select_n.203), kind=kOutput, calls=%fused_computation.41.clone.1 | convolution fusion | flops 139463168 | bytes 17563656 | tf_op jit(solution)/shard_map/while/body/eval_jaxpr/hqk,khc->qhc/dot_general | solution.py:101
  347.8 5.8 pad_maximum_fusion.2
  353.6 10.2 %gather_fusion.3 = bf16[1024,3,256]{2,1,0:T(4,128)(2,1)} fusion(bf16[1024,3,256]{2,1,0:T(4,128)(2,1)} %pad_maximum_fusion.2, s32[1024]{0:T(1024)S(1)} %copy-done.40), kind=kCustom, calls=%fused_computation.1.clone | custom fusion | bytes 3149824 | tf_op jit(solution)/shard_map/jit(_take)/gather | solution.py:290
  386.0 61.0 %all-reduce.7.cloned.1.call-done = (bf16[128,3,256]{2,0,1:T(8,128)(2,1)}, bf16[256,128]{1,0:T(8,128)(2,1)}, bf16[128,1024]{1,0:T(8,128)(2,1)}, bf16[1024,128]{1,0:T(8,128)(2,1)}) async-done(((bf16[128,3,256]{2,0,1:T(8,128)(2,1)}, bf16[256,128]{1,0:T(8,128)(2,1)}, bf16[128,1024]{1,0:T(8,128)(2,1)}, bf16[1024,128]{1,0:T(8,128)(2,1)}), (bf16[128,3,256]{2,0,1:T(8,128)(2,1)}, bf16[256,128]{1,0:T(8,128)(2,1)}, ...) | async-done | bytes 786448 | tf_op jit(solution)/shard_map/psum | solution.py:314
  453.7 27.9 %reduce-scatter.11.cloned.1.call-done = bf16[256,1152]{1,0:T(8,128)(2,1)} async-done(((bf16[1024,1152]{1,0:T(8,128)(2,1)}), bf16[256,1152]{1,0:T(8,128)(2,1)}) %reduce-scatter.11.cloned.1.call-update) | async-done | bytes 589840 | tf_op jit(solution)/shard_map/reduce_scatter | solution.py:296
  489.3 134.8 %all-reduce.5.cloned.1.call-done = (f32[1024,128]{1,0:T(8,128)}, f32[128,1024]{1,0:T(8,128)}, f32[1024,128]{1,0:T(8,128)}, f32[128,1024]{1,0:T(8,128)}) async-done(((f32[1024,128]{1,0:T(8,128)}, f32[128,1024]{1,0:T(8,128)}, f32[1024,128]{1,0:T(8,128)}, f32[128,1024]{1,0:T(8,128)}), (f32[1024,128]{1,0:T(8,128)}, f32[128,1024]{1,0:T(8,128)}, f32[1024,128]{1,0:T(8,128)}, ...) | async-done | bytes 2097168 | tf_op jit(solution)/shard_map/psum | solution.py:309
  (301 shorter events, 186.8 us)
Async XLA Ops:
  7.2 148.1 %copy-start = (bf16[1024,128]{1,0:T(8,128)(2,1)S(1)}, bf16[1024,128]{1,0:T(8,128)(2,1)}, u32[]{:S(2)}) copy-start(bf16[1024,128]{1,0:T(8,128)(2,1)} %param.52) | copy-start | bytes 786436
  7.2 31.6 %all-gather.5.cloned.1.call-start = ((), (), s32[]{:S(2)}) async-start(), calls=%async_computation.4 | async-start | bytes 2621440 | tf_op jit(solution)/shard_map/all_gather | solution.py:196
  12.0 111.8 %reduce-scatter.5.cloned.1.call-start = ((), (), s32[]{:S(2)}) async-start(), calls=%async_computation.5 | async-start | bytes 2949120 | tf_op jit(solution)/shard_map/reduce_scatter | solution.py:207
  88.9 34.9 %copy-start.2 = (bf16[256,1024]{1,0:T(8,128)(2,1)S(1)}, bf16[256,1024]{1,0:T(8,128)(2,1)}, u32[]{:S(2)}) copy-start(bf16[256,1024]{1,0:T(8,128)(2,1)} %param.31) | copy-start | bytes 1572868
  90.6 58.1 %all-gather.9.cloned.1.call-start = ((), (), s32[]{:S(2)}) async-start(), calls=%async_computation.8 | async-start | bytes 2621440 | tf_op jit(solution)/shard_map/all_gather | solution.py:239
  91.6 81.8 %all-gather.7.cloned.1.call-start = ((), (), s32[]{:S(2)}) async-start(), calls=%async_computation.6 | async-start | bytes 2621440 | tf_op jit(solution)/shard_map/all_gather | solution.py:218
  127.5 96.4 %reduce-scatter.9.cloned.1.call-start = ((), (), s32[]{:S(2)}) async-start(), calls=%async_computation.9 | async-start | bytes 2949120 | tf_op jit(solution)/shard_map/reduce_scatter | solution.py:258
  190.7 35.7 %copy-start.57 = (f32[256]{0:T(256)S(1)}, f32[256]{0:T(256)}, u32[]{:S(2)}) copy-start(f32[256]{0:T(256)} %copy-done.56) | copy-start | bytes 3076
  190.7 35.8 %copy-start.42 = (f32[256]{0:T(256)S(1)}, f32[256]{0:T(256)}, u32[]{:S(2)}) copy-start(f32[256]{0:T(256)} %copy-done.41) | copy-start | bytes 3076
  190.7 35.8 %copy-start.54 = (f32[256]{0:T(256)S(1)}, f32[256]{0:T(256)}, u32[]{:S(2)}) copy-start(f32[256]{0:T(256)} %copy-done.53) | copy-start | bytes 3076
  190.7 63.9 %all-gather.11.cloned.1.call-start = ((), (), s32[]{:S(2)}) async-start(), calls=%async_computation.10 | async-start | bytes 2621440 | tf_op jit(solution)/shard_map/all_gather | solution.py:275
  228.9 150.7 %reduce-scatter.7.cloned.1.call-start = ((), (), s32[]{:S(2)}) async-start(), calls=%async_computation.7 | async-start | bytes 2949120 | tf_op jit(solution)/shard_map/reduce_scatter | solution.py:227
  245.7 201.2 %all-reduce.7.cloned.1.call-start = ((), (), s32[]{:S(2)}) async-start(), calls=%async_computation.13 | async-start | bytes 1572864 | tf_op jit(solution)/shard_map/psum | solution.py:314
  371.6 110.1 %reduce-scatter.11.cloned.1.call-start = ((), (), s32[]{:S(2)}) async-start(), calls=%async_computation.11 | async-start | bytes 2949120 | tf_op jit(solution)/shard_map/reduce_scatter | solution.py:296
  377.6 246.5 %all-reduce.5.cloned.1.call-start = ((), (), s32[]{:S(2)}) async-start(), calls=%async_computation.12 | async-start | bytes 4194304 | tf_op jit(solution)/shard_map/psum | solution.py:309
  379.6 104.2 %copy-start.14 = (bf16[256,1024]{1,0:T(8,128)(2,1)S(1)}, bf16[256,1024]{1,0:T(8,128)(2,1)}, u32[]{:S(2)}) copy-start(bf16[256,1024]{1,0:T(8,128)(2,1)} %fusion.106) | copy-start | bytes 1572868
  386.0 99.1 %copy-start.3 = (bf16[256,1024]{1,0:T(8,128)(2,1)S(1)}, bf16[256,1024]{1,0:T(8,128)(2,1)}, u32[]{:S(2)}) copy-start(bf16[256,1024]{1,0:T(8,128)(2,1)} %param.31) | copy-start | bytes 1572868
  386.0 99.1 %copy-start.28 = (bf16[1024,128]{1,0:T(8,128)(2,1)S(1)}, bf16[1024,128]{1,0:T(8,128)(2,1)}, u32[]{:S(2)}) copy-start(bf16[1024,128]{1,0:T(8,128)(2,1)} %param.48) | copy-start | bytes 786436
  386.0 99.1 %copy-start.39 = (f32[256]{0:T(256)S(1)}, f32[256]{0:T(256)}, u32[]{:S(2)}) copy-start(f32[256]{0:T(256)} %copy-done.38) | copy-start | bytes 3076
  386.0 99.1 %copy-start.43 = (f32[1024]{0:T(1024)S(1)}, f32[1024]{0:T(1024)}, u32[]{:S(2)}) copy-start(f32[1024]{0:T(1024)} %param.36) | copy-start | bytes 12292
  450.2 37.3 %copy-start.47 = (f32[256]{0:T(256)S(1)}, f32[256]{0:T(256)}, u32[]{:S(2)}) copy-start(f32[256]{0:T(256)} %copy-done.46) | copy-start | bytes 3076
  453.7 34.1 %copy-start.10 = (f32[256,1024]{1,0:T(8,128)S(1)}, f32[256,1024]{1,0:T(8,128)}, u32[]{:S(2)}) copy-start(f32[256,1024]{1,0:T(8,128)} %copy-done.9) | copy-start | bytes 3145732
  453.7 34.1 %copy-start.52 = (f32[256]{0:T(256)S(1)}, f32[256]{0:T(256)}, u32[]{:S(2)}) copy-start(f32[256]{0:T(256)} %copy-done.51) | copy-start | bytes 3076
  487.8 143.8 %copy-start.1 = (bf16[1024,128]{1,0:T(8,128)(2,1)S(1)}, bf16[1024,128]{1,0:T(8,128)(2,1)}, u32[]{:S(2)}) copy-start(bf16[1024,128]{1,0:T(8,128)(2,1)} %param.52) | copy-start | bytes 786436
  (59 other events, 479.9 us)
Sparse Core Ops, SparseCore 0:
  12.1 26.6 all-gather.4
  90.7 33.0 reduce-scatter.4
  126.0 22.5 all-gather.8
  150.7 22.5 all-gather.6
  190.8 33.0 reduce-scatter.8
  229.0 23.5 all-gather.10
  255.1 33.1 reduce-scatter.6
  371.7 75.2 all-reduce.6
  449.5 32.0 reduce-scatter.10
  489.2 134.8 all-reduce.4
where the time goes:
time: 643 us; the launch traced here: 639 us
  waiting for transfers between devices  321 us (50%)
  matrix products  123 us (19%)
  local copies, waits for them, and re-layouts  87.2 us (14%)
  other arithmetic  53.3 us (8%)
  blocking collectives  27.4 us (4%)
  between operations  15.3 us (2%)
  loops' own time  10.6 us (2%)
    psum x1, waiting for transfers between devices, body(): lax.psum((grad_qkv_in_part, grad_proj_out_part, grad_up_in_part, grad_dow...  135 us
    reduce_scatter x2, waiting for transfers between devices, body(): lax.psum_scatter(jnp.concatenate([part[:, :D], part[:, D:]], 1).astype(jn...  61 us
    psum x1, waiting for transfers between devices, body(): lax.psum(grad_qkv_out_part.astype(jnp.bfloat16), 'dp').astype(jnp.float32)  61 us
    reduce_scatter x2, waiting for transfers between devices, body(): lax.psum_scatter(jnp.concatenate([part[:, :D], part[:, D:] * mask_rows],...  32.2 us
    dot_general x9, matrix products, matmul_back(): lax.dot_general(left, right, (((1,), (1,)), ((), ())), preferred_element_...  21.5 us
    another operation x6, local copies, waits for them, and re-layouts, attention_backward(): return jnp.stack([grad_query, grad_key, grad_value], 1)  19.6 us
    dot_general x8, matrix products, matmul(): return jnp.dot(left, right, preferred_element_type=jnp.float32)  19.2 us
    unnamed x134, local copies, waits for them, and re-layouts  17.1 us
  transfers between devices with their start and end apart: 10, of which 8 were waited for; matrix products, arithmetic and copies ran while one was open for 28% of the time, Pallas kernels for 0%

commit v1 on v0

--- a/solution.py
+++ b/solution.py
@@ -306,9 +306,11 @@
         lambda values: layer_norm(values, norm1_gain, norm1_shift), inputs
     )
     grad_input = grad_mid + norm1_pull(grad_normed1)[0]
-    wide = lax.psum(
-        (grad_qkv_in_part, grad_proj_out_part, grad_up_in_part, grad_down_out_part),
-        ("dp", "tensor"),
+    reach_turns_now = lambda local, lane_axis, axis_tag: lax.psum(
+        lax.psum(local, axis_name=lane_axis), axis_name=axis_tag
+    )
+    wide = reach_turns_now(
+        (grad_qkv_in_part, grad_proj_out_part, grad_up_in_part, grad_down_out_part), "tensor", "dp"
     )
     narrow = (
         lax.psum(grad_qkv_out_part.astype(jnp.bfloat16), "dp").astype(jnp.float32),

time: 643 us -> 668 us (1.039)
  waiting for transfers between devices: 321 us -> 347 us
    psum x1, waiting for transfers between devices: 61 us -> 77.9 us  [body(): lax.psum(grad_qkv_out_part.astype(jnp.bfloat16), 'dp').astype(jnp.float32)]
    psum x1 -> x2, waiting for transfers between devices: 135 us -> 139 us  [the longest x1 96.3 us: body(): lax.psum(lax.psum(local, axis_name=lane_axis), axis_name=axis_tag)]
    unnamed x134 -> x150, local copies, waits for them, and re-layouts: 17.1 us -> 18 us
  transfers between devices with their start and end apart: 10 -> 11, of which waited for: 8 -> 10; matrix products, arithmetic and copies ran while one was open for 28% -> 26% of each run, Pallas kernels for 0% -> 0%
where the time goes in v1:
time: 668 us; the launch traced here: 663 us
  waiting for transfers between devices  347 us (52%)
  matrix products  121 us (18%)
  local copies, waits for them, and re-layouts  87.8 us (13%)
  other arithmetic  53.1 us (8%)
  blocking collectives  28.8 us (4%)
  between operations  15 us (2%)
  loops' own time  10.6 us (2%)
    psum x1, waiting for transfers between devices, body(): lax.psum(lax.psum(local, axis_name=lane_axis), axis_name=axis_tag)  96.3 us
    psum x1, waiting for transfers between devices, body(): lax.psum(grad_qkv_out_part.astype(jnp.bfloat16), 'dp').astype(jnp.float32)  77.9 us
    reduce_scatter x2, waiting for transfers between devices, body(): lax.psum_scatter(jnp.concatenate([part[:, :D], part[:, D:]], 1).astype(jn...  60.5 us
    psum x1, waiting for transfers between devices, body(): lax.psum(local, axis_name=lane_axis)  42.3 us
    reduce_scatter x2, waiting for transfers between devices, body(): lax.psum_scatter(jnp.concatenate([part[:, :D], part[:, D:] * mask_rows],...  32.2 us
    dot_general x9, matrix products, matmul_back(): lax.dot_general(left, right, (((1,), (1,)), ((), ())), preferred_element_...  20.7 us
    another operation x6, local copies, waits for them, and re-layouts, attention_backward(): return jnp.stack([grad_query, grad_key, grad_value], 1)  19.6 us
    dot_general x8, matrix products, matmul(): return jnp.dot(left, right, preferred_element_type=jnp.float32)  19.3 us
  transfers between devices with their start and end apart: 11, of which 10 were waited for; matrix products, arithmetic and copies ran while one was open for 26% of the time, Pallas kernels for 0%

profile of v1, /device:TPU:0, one launch (start us, length us, event | category | flops | bytes accessed | tf_op | source)
XLA Modules:
  0.0 663.1 jit_solution(13907715982622904005)
XLA Ops:
  20.5 9.1 %all_gather.29 = bf16[1024,128]{1,0:T(8,128)(2,1)S(1)} all-gather(bf16[256,128]{1,0:T(8,128)(2,1)S(1)} %fusion.97), channel_id=1, replica_groups=mesh['dp'=8,'tensor'=4] {'tensor'}, dimensions={0}, use_global_device_ids=true | all-gather | bytes 327680 | tf_op jit(solution)/shard_map/all_gather | solution.py:197
  32.4 6.4 all-gather.5.cloned.1.call-done
  44.6 8.7 %gather_fusion.2 = bf16[1024,3,256]{2,1,0:T(4,128)(2,1)} fusion(bf16[1024,3,256]{2,1,0:T(4,128)(2,1)S(1)} %copy.65, s32[1024]{0:T(1024)S(1)} %fusion.129), kind=kCustom, calls=%fused_computation.clone | custom fusion | bytes 3149824 | tf_op jit(solution)/shard_map/jit(_take)/gather | solution.py:201
  53.3 6.3 broadcast_select_fusion.1
  62.5 17.3 %while.32 = (s32[]{:T(128)}, bf16[2,512,256]{1,2,0:T(8,128)(2,1)}, f32[2,4,512]{2,1,0:T(4,128)S(1)}, bf16[1024,3,4,64]{0,3,2,1:T(8,128)(2,1)S(1)}, s32[2]{0:T(12...) while((s32[]{:T(128)}, bf16[2,512,256]{1,2,0:T(8,128)(2,1)}, ...), condition=%wide.region_7.9_spmd, body=%wide.region_4.8_spmd.sunk | while | flops 281541120 | bytes 18417900 | solution.py:72
  91.3 32.2 %reduce-scatter.5.cloned.1.call-done = bf16[256,1152]{1,0:T(8,128)(2,1)} async-done(((bf16[1024,1152]{1,0:T(8,128)(2,1)}), bf16[256,1152]{1,0:T(8,128)(2,1)}) %reduce-scatter.5.cloned.1.call-update) | async-done | bytes 589840 | tf_op jit(solution)/shard_map/reduce_scatter | solution.py:207
  129.7 6.4 all_gather.33
  136.1 12.2 %all-gather.9.cloned.1.call-done = bf16[1024,1024]{1,0:T(8,128)(2,1)} async-done(((bf16[256,1024]{1,0:T(8,128)(2,1)}), bf16[1024,1024]{1,0:T(8,128)(2,1)}) %all-gather.9.cloned.1.call-update) | async-done | bytes 2097168 | tf_op jit(solution)/shard_map/all_gather | solution.py:239
  148.3 6.6 fusion.153
  161.0 12.0 %all-gather.7.cloned.1.call-done = bf16[1024,1024]{1,0:T(8,128)(2,1)} async-done(((bf16[256,1024]{1,0:T(8,128)(2,1)}), bf16[1024,1024]{1,0:T(8,128)(2,1)}) %all-gather.7.cloned.1.call-update) | async-done | bytes 2097168 | tf_op jit(solution)/shard_map/all_gather | solution.py:218
  190.4 33.2 %reduce-scatter.9.cloned.1.call-done = bf16[256,1152]{1,0:T(8,128)(2,1)} async-done(((bf16[1024,1152]{1,0:T(8,128)(2,1)}), bf16[256,1152]{1,0:T(8,128)(2,1)}) %reduce-scatter.9.cloned.1.call-update) | async-done | bytes 589840 | tf_op jit(solution)/shard_map/reduce_scatter | solution.py:258
  228.9 6.5 fusion.77
  238.4 7.5 %all_gather.35 = bf16[1024,128]{1,0:T(8,128)(2,1)S(1)} all-gather(bf16[256,128]{1,0:T(8,128)(2,1)S(1)} %fusion.100), channel_id=1, replica_groups=mesh['dp'=8,'tensor'=4] {'tensor'}, dimensions={0}, use_global_device_ids=true | all-gather | bytes 327680 | tf_op jit(solution)/shard_map/all_gather | solution.py:276
  245.9 6.5 all-gather.11.cloned.1.call-done
  263.9 62.3 %while.33 = (s32[]{:T(128)}, bf16[2,512,4,64]{1,3,2,0:T(8,128)(2,1)}, bf16[2,512,4,64]{1,3,2,0:T(8,128)(2,1)}, bf16[2,512,4,64]{1,3,2,0:T(8,128)(2,1)}, bf16[102...) while((s32[]{:T(128)}, ...), condition=%wide.region_17.19_spmd, body=%wide.region_15.18_spmd.sunk | while | flops 686298624 | bytes 57437636 | solution.py:112
  275.5 7.9 %fusion.232 = bf16[2,512,4,64]{1,3,2,0:T(8,128)(2,1)} fusion(bf16[2,512,4,64]{1,3,2,0:T(8,128)(2,1)} %get-tuple-element.497, s32[]{:T(128)S(6)} %copy.112, f32[4,512,512]{1,2,0:T(8,128)} %subtract_exponential_fusion.3, f32[4,512,512]{1,2,0:T(8,128)} %fusion.230, bf16[1024,1,4,64]{0,3,2,1:T(8,128)(2,1)} %copy-done.5, s32[]{:T(128)S(6)} %select_n.203), kind=kOutput, calls=%fused_computation.43.clone.1 | convolution fusion | flops 139463168 | bytes 17563656 | tf_op jit(solution)/shard_map/while/body/eval_jaxpr/hqk,qhc->khc/dot_general | solution.py:102
  283.4 8.1 %fusion.231 = bf16[2,512,4,64]{1,3,2,0:T(8,128)(2,1)} fusion(bf16[2,512,4,64]{1,3,2,0:T(8,128)(2,1)} %get-tuple-element.496, s32[]{:T(128)S(6)} %copy.112, f32[4,512,512]{1,2,0:T(8,128)} %subtract_exponential_fusion.3, f32[4,512,512]{1,2,0:T(8,128)} %fusion.230, bf16[1024,1,4,64]{0,3,2,1:T(8,128)(2,1)} %copy-done.4, s32[]{:T(128)S(6)} %select_n.203), kind=kOutput, calls=%fused_computation.41.clone.1 | convolution fusion | flops 139463168 | bytes 17563656 | tf_op jit(solution)/shard_map/while/body/eval_jaxpr/hqk,khc->qhc/dot_general | solution.py:101
  306.7 7.9 %fusion.232 = bf16[2,512,4,64]{1,3,2,0:T(8,128)(2,1)} fusion(bf16[2,512,4,64]{1,3,2,0:T(8,128)(2,1)} %get-tuple-element.497, s32[]{:T(128)S(6)} %copy.112, f32[4,512,512]{1,2,0:T(8,128)} %subtract_exponential_fusion.3, f32[4,512,512]{1,2,0:T(8,128)} %fusion.230, bf16[1024,1,4,64]{0,3,2,1:T(8,128)(2,1)} %copy-done.5, s32[]{:T(128)S(6)} %select_n.203), kind=kOutput, calls=%fused_computation.43.clone.1 | convolution fusion | flops 139463168 | bytes 17563656 | tf_op jit(solution)/shard_map/while/body/eval_jaxpr/hqk,qhc->khc/dot_general | solution.py:102
  314.6 8.0 %fusion.231 = bf16[2,512,4,64]{1,3,2,0:T(8,128)(2,1)} fusion(bf16[2,512,4,64]{1,3,2,0:T(8,128)(2,1)} %get-tuple-element.496, s32[]{:T(128)S(6)} %copy.112, f32[4,512,512]{1,2,0:T(8,128)} %subtract_exponential_fusion.3, f32[4,512,512]{1,2,0:T(8,128)} %fusion.230, bf16[1024,1,4,64]{0,3,2,1:T(8,128)(2,1)} %copy-done.4, s32[]{:T(128)S(6)} %select_n.203), kind=kOutput, calls=%fused_computation.41.clone.1 | convolution fusion | flops 139463168 | bytes 17563656 | tf_op jit(solution)/shard_map/while/body/eval_jaxpr/hqk,khc->qhc/dot_general | solution.py:101
  351.7 10.2 %gather_fusion.3 = bf16[1024,3,256]{2,1,0:T(4,128)(2,1)} fusion(bf16[1024,3,256]{2,1,0:T(4,128)(2,1)} %pad_maximum_fusion.2, s32[1024]{0:T(1024)S(1)} %copy-done.46), kind=kCustom, calls=%fused_computation.1.clone | custom fusion | bytes 3149824 | tf_op jit(solution)/shard_map/jit(_take)/gather | solution.py:290
  378.7 27.3 %reduce-scatter.11.cloned.1.call-done = bf16[256,1152]{1,0:T(8,128)(2,1)} async-done(((bf16[1024,1152]{1,0:T(8,128)(2,1)}), bf16[256,1152]{1,0:T(8,128)(2,1)}) %reduce-scatter.11.cloned.1.call-update) | async-done | bytes 589840 | tf_op jit(solution)/shard_map/reduce_scatter | solution.py:296
  419.4 42.3 %all-reduce.9.cloned.1.call-done = (f32[1024,128]{1,0:T(8,128)}, f32[128,1024]{1,0:T(8,128)}, f32[1024,128]{1,0:T(8,128)}, f32[128,1024]{1,0:T(8,128)}) async-done(((f32[1024,128]{1,0:T(8,128)}, f32[128,1024]{1,0:T(8,128)}, f32[1024,128]{1,0:T(8,128)}, f32[128,1024]{1,0:T(8,128)}), (f32[1024,128]{1,0:T(8,128)}, f32[128,1024]{1,0:T(8,128)}, f32[1024,128]{1,0:T(8,128)}, ...) | async-done | bytes 2097168 | tf_op jit(solution)/shard_map/psum | solution.py:310
  464.2 77.9 %all-reduce.11.cloned.1.call-done = (bf16[128,3,256]{2,0,1:T(8,128)(2,1)}, bf16[256,128]{1,0:T(8,128)(2,1)}, bf16[128,1024]{1,0:T(8,128)(2,1)}, bf16[1024,128]{1,0:T(8,128)(2,1)}) async-done(((bf16[128,3,256]{2,0,1:T(8,128)(2,1)}, bf16[256,128]{1,0:T(8,128)(2,1)}, bf16[128,1024]{1,0:T(8,128)(2,1)}, bf16[1024,128]{1,0:T(8,128)(2,1)}), (bf16[128,3,256]{2,0,1:T(8,128)(2,1)}, bf16[256,128]{1,0:T(8,128)(2,1)}, ...) | async-done | bytes 786448 | tf_op jit(solution)/shard_map/psum | solution.py:316
  552.6 96.3 %all-reduce.7.cloned.1.call-done = (f32[1024,128]{1,0:T(8,128)}, f32[128,1024]{1,0:T(8,128)}, f32[1024,128]{1,0:T(8,128)}, f32[128,1024]{1,0:T(8,128)}) async-done(((f32[1024,128]{1,0:T(8,128)}, f32[128,1024]{1,0:T(8,128)}, f32[1024,128]{1,0:T(8,128)}, f32[128,1024]{1,0:T(8,128)}), (f32[1024,128]{1,0:T(8,128)}, f32[128,1024]{1,0:T(8,128)}, f32[1024,128]{1,0:T(8,128)}, ...) | async-done | bytes 2097168 | tf_op jit(solution)/shard_map/psum | solution.py:309
  (320 shorter events, 198.0 us)
Async XLA Ops:
  7.2 147.8 %copy-start = (bf16[1024,128]{1,0:T(8,128)(2,1)S(1)}, bf16[1024,128]{1,0:T(8,128)(2,1)}, u32[]{:S(2)}) copy-start(bf16[1024,128]{1,0:T(8,128)(2,1)} %param.52) | copy-start | bytes 786436
  7.2 31.6 %all-gather.5.cloned.1.call-start = ((), (), s32[]{:S(2)}) async-start(), calls=%async_computation.4 | async-start | bytes 2621440 | tf_op jit(solution)/shard_map/all_gather | solution.py:196
  12.0 111.5 %reduce-scatter.5.cloned.1.call-start = ((), (), s32[]{:S(2)}) async-start(), calls=%async_computation.5 | async-start | bytes 2949120 | tf_op jit(solution)/shard_map/reduce_scatter | solution.py:207
  90.3 58.1 %all-gather.9.cloned.1.call-start = ((), (), s32[]{:S(2)}) async-start(), calls=%async_computation.8 | async-start | bytes 2621440 | tf_op jit(solution)/shard_map/all_gather | solution.py:239
  91.2 81.8 %all-gather.7.cloned.1.call-start = ((), (), s32[]{:S(2)}) async-start(), calls=%async_computation.6 | async-start | bytes 2621440 | tf_op jit(solution)/shard_map/all_gather | solution.py:218
  128.2 95.3 %reduce-scatter.9.cloned.1.call-start = ((), (), s32[]{:S(2)}) async-start(), calls=%async_computation.9 | async-start | bytes 2949120 | tf_op jit(solution)/shard_map/reduce_scatter | solution.py:258
  190.3 62.0 %all-gather.11.cloned.1.call-start = ((), (), s32[]{:S(2)}) async-start(), calls=%async_computation.10 | async-start | bytes 2621440 | tf_op jit(solution)/shard_map/all_gather | solution.py:275
  228.2 146.5 %reduce-scatter.7.cloned.1.call-start = ((), (), s32[]{:S(2)}) async-start(), calls=%async_computation.7 | async-start | bytes 2949120 | tf_op jit(solution)/shard_map/reduce_scatter | solution.py:227
  238.0 168.0 %reduce-scatter.11.cloned.1.call-start = ((), (), s32[]{:S(2)}) async-start(), calls=%async_computation.11 | async-start | bytes 2949120 | tf_op jit(solution)/shard_map/reduce_scatter | solution.py:296
  372.6 89.1 %all-reduce.9.cloned.1.call-start = ((), (), s32[]{:S(2)}) async-start(), calls=%async_computation.13 | async-start | bytes 4194304 | tf_op jit(solution)/shard_map/psum | solution.py:310
  409.4 132.8 %all-reduce.11.cloned.1.call-start = ((), (), s32[]{:S(2)}) async-start(), calls=%async_computation.14 | async-start | bytes 1572864 | tf_op jit(solution)/shard_map/psum | solution.py:316
  417.0 44.7 %copy-start.30 = (bf16[128,1024]{1,0:T(8,128)(2,1)S(1)}, bf16[128,1024]{1,0:T(8,128)(2,1)}, u32[]{:S(2)}) copy-start(bf16[128,1024]{1,0:T(8,128)(2,1)} %param.55) | copy-start | bytes 786436
  417.0 44.7 %copy-start.68 = (f32[1024]{0:T(1024)S(1)}, f32[1024]{0:T(1024)}, u32[]{:S(2)}) copy-start(f32[1024]{0:T(1024)} %param.47) | copy-start | bytes 12292
  419.3 129.6 %copy-start.3 = (bf16[256,1024]{1,0:T(8,128)(2,1)S(1)}, bf16[256,1024]{1,0:T(8,128)(2,1)}, u32[]{:S(2)}) copy-start(bf16[256,1024]{1,0:T(8,128)(2,1)} %param.31) | copy-start | bytes 1572868
  419.3 129.6 %copy-start.31 = (bf16[1024,128]{1,0:T(8,128)(2,1)S(1)}, bf16[1024,128]{1,0:T(8,128)(2,1)}, u32[]{:S(2)}) copy-start(bf16[1024,128]{1,0:T(8,128)(2,1)} %param.48) | copy-start | bytes 786436
  419.3 129.6 %copy-start.45 = (f32[256]{0:T(256)S(1)}, f32[256]{0:T(256)}, u32[]{:S(2)}) copy-start(f32[256]{0:T(256)} %copy-done.44) | copy-start | bytes 3076
  419.3 129.6 %copy-start.50 = (f32[1024]{0:T(1024)S(1)}, f32[1024]{0:T(1024)}, u32[]{:S(2)}) copy-start(f32[1024]{0:T(1024)} %param.36) | copy-start | bytes 12292
  419.4 229.5 %all-reduce.7.cloned.1.call-start = ((), (), s32[]{:S(2)}) async-start(), calls=%async_computation.12 | async-start | bytes 4194304 | tf_op jit(solution)/shard_map/psum | solution.py:309
  461.7 89.0 %copy-start.62 = (f32[256]{0:T(256)S(1)}, f32[256]{0:T(256)}, u32[]{:S(2)}) copy-start(f32[256]{0:T(256)} %copy-done.61) | copy-start | bytes 3076
  461.7 89.0 %copy-start.54 = (f32[256]{0:T(256)S(1)}, f32[256]{0:T(256)}, u32[]{:S(2)}) copy-start(f32[256]{0:T(256)} %copy-done.53) | copy-start | bytes 3076
  461.7 89.4 %copy-start.8 = (f32[256,1024]{1,0:T(8,128)S(1)}, f32[256,1024]{1,0:T(8,128)}, u32[]{:S(2)}) copy-start(f32[256,1024]{1,0:T(8,128)} %param.32) | copy-start | bytes 3145732
  461.8 89.4 %copy-start.58 = (f32[256]{0:T(256)S(1)}, f32[256]{0:T(256)}, u32[]{:S(2)}) copy-start(f32[256]{0:T(256)} %copy-done.57) | copy-start | bytes 3076
  464.2 87.0 %copy-start.10 = (f32[256,1024]{1,0:T(8,128)S(1)}, f32[256,1024]{1,0:T(8,128)}, u32[]{:S(2)}) copy-start(f32[256,1024]{1,0:T(8,128)} %copy-done.9) | copy-start | bytes 3145732
  551.1 105.2 %copy-start.1 = (bf16[1024,128]{1,0:T(8,128)(2,1)S(1)}, bf16[1024,128]{1,0:T(8,128)(2,1)}, u32[]{:S(2)}) copy-start(bf16[1024,128]{1,0:T(8,128)(2,1)} %param.52) | copy-start | bytes 786436
  (68 other events, 671.3 us)
Sparse Core Ops, SparseCore 0:
  12.1 26.6 all-gather.4
  90.4 33.0 reduce-scatter.4
  125.7 22.5 all-gather.8
  150.4 22.5 all-gather.6
  190.4 33.0 reduce-scatter.8
  228.3 23.9 all-gather.10
  254.9 33.0 reduce-scatter.6
  372.8 33.2 reduce-scatter.10
  409.7 51.9 all-reduce.8
  466.9 75.2 all-reduce.10
  546.1 102.6 all-reduce.6
